TPU v7x, 32 devices: a whole 2x2x4 slice. The times are simulated.
32 devices in a mesh: gx: 4 (over y, core), gy: 8 (over z, x).
Axes of the slice: x: 2, y: 2, z: 4, core: 2. Of those that a mesh axis runs over, the one named last changes fastest.
Arguments:
- tokens: bfloat16 [4, 256, 6144], P('gx', None, 'gy'), may hold values from -6 to 6
- norm_gain: float32 [6144], replicated, may hold values from 0.1 to 1.9
- qkv_weight: bfloat16 [6144, 3, 4096], P('gx', None, 'gy'), may hold values from -0.078125 to 0.078125
- up_weight: bfloat16 [6144, 24576], P('gx', 'gy'), may hold values from -0.078125 to 0.078125
- query_gain: float32 [128], replicated, may hold values from 0.1 to 1.9
- key_gain: float32 [128], replicated, may hold values from 0.1 to 1.9
- out_weight: bfloat16 [4096, 6144], P('gy', 'gx'), may hold values from -0.09375 to 0.09375
- down_weight: bfloat16 [24576, 6144], P('gy', 'gx'), may hold values from -0.0390625 to 0.0390625
- attention_keep: int32 [4, 256, 6144], P('gx', None, 'gy'), may hold values 0 or 1
- feedforward_keep: int32 [4, 256, 6144], P('gx', None, 'gy'), may hold values 0 or 1
Outputs:
- block_out: bfloat16 [4, 256, 6144], P('gx', None, 'gy')
All inputs are finite; a program needn't handle non-finite values. No bound on the sum of `attention_keep` or of `feedforward_keep` on one device may be relied on, other than what follows from the above.
Results may differ from a plain program's by a relative error of at most 0.017.
Values may be sent and summed in bfloat16 or wider, within the bound.
A program may use at most 128 MiB of HBM per device.

v0:
```python
import jax
import jax.numpy as jnp
from jax import lax
from jax.sharding import PartitionSpec as P

epsilon = 1e-06
keep_scale = 1.0 / 0.9


def layer_norm(values, gain):
    center = values - jnp.mean(values, axis=-1, keepdims=True)
    variance = jnp.mean(center * center, axis=-1, keepdims=True)
    return center * lax.rsqrt(variance + epsilon) * gain


def head_norm(values, gain):
    row_count = values.shape[0]
    shaped = values.reshape(row_count, -1, gain.shape[0])
    return layer_norm(shaped, gain).reshape(row_count, -1)


def per_device(
    tokens,
    norm_gain,
    qkv_weight,
    up_weight,
    query_gain,
    key_gain,
    out_weight,
    down_weight,
    attention_keep,
    feedforward_keep,
):
    images, seq_len, slice_width = tokens.shape
    whole_rows = lax.all_gather(tokens, "gy", axis=2, tiled=True)
    model_width = whole_rows.shape[2]
    own_rows = images * seq_len
    normed = (
        layer_norm(whole_rows.astype(jnp.float32), norm_gain)
        .astype(jnp.bfloat16)
        .reshape(own_rows, model_width)
    )
    blocks = lax.all_to_all(normed, "gx", split_axis=1, concat_axis=0, tiled=True)
    block_width = blocks.shape[1]
    head_cols = qkv_weight.shape[2]
    head_size = query_gain.shape[0]
    qkv_flat = qkv_weight.reshape(block_width, 3 * head_cols)
    joined = jnp.concatenate([qkv_flat, up_weight], axis=1)
    united = lax.psum_scatter(
        jnp.dot(blocks, joined, preferred_element_type=jnp.float32).astype(jnp.bfloat16),
        "gx",
        scatter_dimension=0,
        tiled=True,
    ).astype(jnp.float32)
    queries = head_norm(united[:, :head_cols], query_gain).astype(jnp.bfloat16)
    keys = head_norm(united[:, head_cols : 2 * head_cols], key_gain).astype(jnp.bfloat16)
    values = united[:, 2 * head_cols : 3 * head_cols].astype(jnp.bfloat16)
    hidden = jax.nn.gelu(united[:, 3 * head_cols :], approximate=False).astype(jnp.bfloat16)
    query_grid = queries.reshape(images, seq_len, -1, head_size)
    key_grid = keys.reshape(images, seq_len, -1, head_size)
    value_grid = values.reshape(images, seq_len, -1, head_size)
    scores = jnp.einsum(
        "bshd,bthd->bhst", query_grid, key_grid, preferred_element_type=jnp.float32
    ) * head_size ** (-0.5)
    raised = jnp.exp(scores)
    weights = (raised / jnp.sum(raised, axis=-1, keepdims=True)).astype(jnp.bfloat16)
    attended = jnp.einsum(
        "bhst,bthd->bshd", weights, value_grid, preferred_element_type=jnp.float32
    )
    attended = attended.astype(jnp.bfloat16).reshape(own_rows, head_cols)
    attention_part = jnp.dot(
        lax.all_gather(attended, "gx", axis=0, tiled=True),
        out_weight,
        preferred_element_type=jnp.float32,
    )
    feedforward_part = jnp.dot(
        lax.all_gather(hidden, "gx", axis=0, tiled=True),
        down_weight,
        preferred_element_type=jnp.float32,
    )
    delivered = (
        lax.all_to_all(
            attention_part.astype(jnp.bfloat16), "gx", split_axis=0, concat_axis=1, tiled=True
        ),
        lax.all_to_all(
            feedforward_part.astype(jnp.bfloat16), "gx", split_axis=0, concat_axis=1, tiled=True
        ),
    )
    rounded = jnp.stack([delivered[0], delivered[1]])
    rounded = lax.optimization_barrier(rounded)
    totals = lax.psum_scatter(
        rounded.astype(jnp.float32).astype(jnp.bfloat16), "gy", scatter_dimension=2, tiled=True
    ).astype(jnp.float32)
    attention_out = totals[0].reshape(images, seq_len, slice_width)
    feedforward_out = totals[1].reshape(images, seq_len, slice_width)
    branches = (
        attention_keep.astype(jnp.float32) * attention_out
        + feedforward_keep.astype(jnp.float32) * feedforward_out
    )
    return (tokens.astype(jnp.float32) + branches * keep_scale).astype(jnp.bfloat16)


def solution(mesh):
    in_specs = (
        P("gx", None, "gy"),
        P(),
        P("gx", None, "gy"),
        P("gx", "gy"),
        P(),
        P(),
        P("gy", "gx"),
        P("gy", "gx"),
        P("gx", None, "gy"),
        P("gx", None, "gy"),
    )
    out_specs = P("gx", None, "gy")
    return jax.shard_map(
        per_device, mesh=mesh, in_specs=in_specs, out_specs=out_specs, check_vma=False
    )
```

profile of v0, /device:TPU:0, one launch (start us, length us, event | category | flops | bytes accessed | tf_op | source)
XLA Modules:
  0.0 534.5 jit_solution(1531559722905003716)
XLA Ops:
  8.6 63.7 %all-gather.4.cloned.1.call-done = bf16[1,256,6144]{1,2,0:T(8,128)(2,1)} async-done(((bf16[1,256,768]{1,2,0:T(8,128)(2,1)}), bf16[1,256,6144]{1,2,0:T(8,128)(2,1)}) %all-gather.4.cloned.1.call-update) | async-done | bytes 3145744 | tf_op jit(solution)/shard_map/all_gather | solution.py:35
  72.3 2.9 convert_reduce_fusion
  76.1 2.3 fusion.11
  78.3 4.7 all-to-all-start
  83.1 6.6 %copy.28 = bf16[1536,3,512]{0,2,1:T(8,128)(2,1)} copy(bf16[1536,3,512]{2,0,1:T(8,128)(2,1)} %param.12) | data formatting | bytes 9437184 | tf_op args[2]
  89.7 6.6 %copy.29 = bf16[1536,1536]{1,0:T(8,128)(2,1)} copy(bf16[1536,1536]{0,1:T(8,128)(2,1)} %bitcast.67) | data formatting | bytes 9437184 | tf_op jit(solution)/shard_map/reshape | solution.py:47
  96.3 23.7 %all-to-all-done = bf16[256,4,1536]{0,2,1:T(8,128)(2,1)} async-done(((bf16[256,4,1536]{0,2,1:T(8,128)(2,1)}), bf16[256,4,1536]{0,2,1:T(8,128)(2,1)}, u32[]{:S(2)}, u32[]{:S(2)}) %all-to-all-start) | async-done | bytes 3145760 | tf_op jit(solution)/shard_map/all_to_all | solution.py:43
  120.0 4.7 copy.27
  124.6 22.6 %fusion.4 = bf16[1024,4608]{1,0:T(8,128)(2,1)} fusion(bf16[1024,1536]{1,0:T(8,128)(2,1)} %bitcast.71, bf16[1536,3072]{1,0:T(8,128)(2,1)} %param.13, bf16[1536,1536]{1,0:T(8,128)(2,1)} %copy.29), kind=kOutput, calls=%fused_computation.4 | convolution fusion | flops 14528544768 | bytes 26738688 | tf_op jit(solution)/shard_map/dot_general | solution.py:50
  148.0 75.2 %reduce-scatter.3.cloned.1.call-done = bf16[256,4608]{1,0:T(8,128)(2,1)} async-done(((bf16[1024,4608]{1,0:T(8,128)(2,1)}), bf16[256,4608]{1,0:T(8,128)(2,1)}) %reduce-scatter.3.cloned.1.call-update) | async-done | bytes 2359312 | tf_op jit(solution)/shard_map/reduce_scatter | solution.py:49
  232.7 8.6 %fusion.14 = bf16[256,3072]{1,0:T(8,128)(2,1)} fusion(f32[256,4608]{1,0:T(8,128)} %copy-done.3), kind=kLoop, calls=%fused_computation.18 | loop fusion | flops 51118080 | bytes 4718592 | tf_op jit(solution)/shard_map/convert_element_type | solution.py:58
  241.3 8.3 %all-gather.6.cloned.1.call-done = bf16[1024,512]{0,1:T(8,128)(2,1)} async-done(((bf16[256,512]{0,1:T(8,128)(2,1)}), bf16[1024,512]{0,1:T(8,128)(2,1)}) %all-gather.6.cloned.1.call-update) | async-done | bytes 1048592 | tf_op jit(solution)/shard_map/all_gather | solution.py:72
  249.6 4.7 convolution_convert_fusion.1
  254.3 4.7 all-to-all-start.1
  259.1 72.0 %all-gather.8.cloned.1.call-done = bf16[1024,3072]{1,0:T(8,128)(2,1)} async-done(((bf16[256,3072]{1,0:T(8,128)(2,1)}), bf16[1024,3072]{1,0:T(8,128)(2,1)}) %all-gather.8.cloned.1.call-update) | async-done | bytes 6291472 | tf_op jit(solution)/shard_map/all_gather | solution.py:77
  331.1 15.6 %convolution_convert_fusion = bf16[1024,1536]{1,0:T(8,128)(2,1)} fusion(bf16[1024,3072]{1,0:T(8,128)(2,1)} %all-gather.8.cloned.1.call-done, bf16[3072,1536]{1,0:T(8,128)(2,1)} %param.17), kind=kOutput, calls=%fused_computation.14 | convolution fusion | flops 9665249280 | bytes 18874368 | tf_op jit(solution)/shard_map/dot_general | solution.py:76
  346.6 4.9 all-to-all-start.2
  351.6 6.0 %copy.34 = bf16[256,4,1536]{2,1,0:T(4,128)(2,1)} copy(bf16[256,4,1536]{2,0,1:T(8,128)(2,1)} %bitcast.11) | data formatting | bytes 6291456 | tf_op jit(solution)/shard_map/all_to_all | solution.py:82
  357.6 6.9 %stack.9 = bf16[1,256,6144]{2,1,0:T(8,128)(2,1)} reshape(bf16[256,4,1536]{2,1,0:T(4,128)(2,1)} %copy.34) | data formatting | bytes 6291456 | tf_op jit(solution)/shard_map/stack | solution.py:89
  364.5 24.0 %all-to-all-done.2 = bf16[4,256,1536]{2,1,0:T(8,128)(2,1)} async-done(((bf16[4,256,1536]{2,1,0:T(8,128)(2,1)}), bf16[4,256,1536]{2,1,0:T(8,128)(2,1)}, u32[]{:S(2)}, u32[]{:S(2)}) %all-to-all-start.2) | async-done | bytes 3145760 | tf_op jit(solution)/shard_map/all_to_all | solution.py:85
  388.5 6.0 %copy.35 = bf16[256,4,1536]{2,1,0:T(4,128)(2,1)} copy(bf16[256,4,1536]{2,0,1:T(8,128)(2,1)} %bitcast.13) | data formatting | bytes 6291456 | tf_op jit(solution)/shard_map/all_to_all | solution.py:85
  394.5 6.9 %stack.10 = bf16[1,256,6144]{2,1,0:T(8,128)(2,1)} reshape(bf16[256,4,1536]{2,1,0:T(4,128)(2,1)} %copy.35) | data formatting | bytes 6291456 | tf_op jit(solution)/shard_map/stack | solution.py:89
  401.4 6.1 %pad_maximum_fusion = bf16[2,256,6144]{2,1,0:T(8,128)(2,1)} fusion(bf16[1,256,6144]{2,1,0:T(8,128)(2,1)} %stack.10, bf16[1,256,6144]{2,1,0:T(8,128)(2,1)} %stack.9), kind=kLoop, calls=%fused_computation.12 | loop fusion | flops 3145728 | bytes 12582912 | tf_op jit(solution)/shard_map/stack | solution.py:89
  407.5 118.2 %reduce-scatter.5.cloned.1.call-done = bf16[2,256,768]{2,1,0:T(8,128)(2,1)} async-done(((bf16[2,256,6144]{2,1,0:T(8,128)(2,1)}), bf16[2,256,768]{2,1,0:T(8,128)(2,1)}) %reduce-scatter.5.cloned.1.call-update) | async-done | bytes 786448 | tf_op jit(solution)/shard_map/reduce_scatter | solution.py:91
  (60 shorter events, 15.4 us)
Async XLA Ops:
  6.5 243.1 %copy-start = (bf16[512,1536]{1,0:T(8,128)(2,1)S(1)}, bf16[512,1536]{1,0:T(8,128)(2,1)}, u32[]{:S(2)}) copy-start(bf16[512,1536]{1,0:T(8,128)(2,1)} %param.16) | copy-start | bytes 4718596
  6.5 65.7 %all-gather.4.cloned.1.call-start = ((), (), s32[]{:S(2)}) async-start(), calls=%async_computation.5 | async-start | bytes 3538944 | tf_op jit(solution)/shard_map/all_gather | solution.py:35
  72.3 2.9 copy-start.2
  72.3 3.8 copy-start.7
  78.3 41.7 %all-to-all-start = ((bf16[256,4,1536]{0,2,1:T(8,128)(2,1)}), bf16[256,4,1536]{0,2,1:T(8,128)(2,1)}, u32[]{:S(2)}, u32[]{:S(2)}) async-start(bf16[256,4,1536]{0,2,1:T(8,128)(2,1)} %bitcast.68), calls=%async_computation | async-start | bytes 6291456 | tf_op jit(solution)/shard_map/all_to_all | solution.py:43
  83.0 140.2 %reduce-scatter.3.cloned.1.call-start = ((), (), s32[]{:S(2)}) async-start(), calls=%async_computation.6 | async-start | bytes 11796480 | tf_op jit(solution)/shard_map/reduce_scatter | solution.py:49
  147.3 0.7 copy-start.8
  147.3 0.7 copy-start.9
  147.3 102.3 %all-gather.6.cloned.1.call-start = ((), (), s32[]{:S(2)}) async-start(), calls=%async_computation.7 | async-start | bytes 1310720 | tf_op jit(solution)/shard_map/all_gather | solution.py:72
  224.3 2.5 slice-start
  229.2 2.1 copy-start.3
  232.7 98.4 %all-gather.8.cloned.1.call-start = ((), (), s32[]{:S(2)}) async-start(), calls=%async_computation.8 | async-start | bytes 7864320 | tf_op jit(solution)/shard_map/all_gather | solution.py:77
  254.3 92.3 %all-to-all-start.1 = ((bf16[4,256,1536]{2,1,0:T(8,128)(2,1)}), bf16[4,256,1536]{2,1,0:T(8,128)(2,1)}, u32[]{:S(2)}, u32[]{:S(2)}) async-start(bf16[4,256,1536]{2,1,0:T(8,128)(2,1)} %bitcast.70), calls=%async_computation.2 | async-start | bytes 6291456 | tf_op jit(solution)/shard_map/all_to_all | solution.py:82
  346.6 41.8 %all-to-all-start.2 = ((bf16[4,256,1536]{2,1,0:T(8,128)(2,1)}), bf16[4,256,1536]{2,1,0:T(8,128)(2,1)}, u32[]{:S(2)}, u32[]{:S(2)}) async-start(bf16[4,256,1536]{2,1,0:T(8,128)(2,1)} %bitcast.69), calls=%async_computation.3 | async-start | bytes 6291456 | tf_op jit(solution)/shard_map/all_to_all | solution.py:85
  351.5 174.2 %reduce-scatter.5.cloned.1.call-start = ((), (), s32[]{:S(2)}) async-start(), calls=%async_computation.9 | async-start | bytes 7077888 | tf_op jit(solution)/shard_map/reduce_scatter | solution.py:91
  407.5 119.4 %copy-start.4 = (bf16[1,256,768]{2,1,0:T(8,128)(2,1)S(1)}, bf16[1,256,768]{2,1,0:T(8,128)(2,1)}, u32[]{:S(2)}) copy-start(bf16[1,256,768]{2,1,0:T(8,128)(2,1)} %param.10) | copy-start | bytes 1179652
  407.5 119.5 %copy-start.5 = (s32[1,256,768]{2,1,0:T(8,128)S(1)}, s32[1,256,768]{2,1,0:T(8,128)}, u32[]{:S(2)}) copy-start(s32[1,256,768]{2,1,0:T(8,128)} %param.19) | copy-start | bytes 2359300
  407.5 119.5 %copy-start.6 = (s32[1,256,768]{2,1,0:T(8,128)S(1)}, s32[1,256,768]{2,1,0:T(8,128)}, u32[]{:S(2)}) copy-start(s32[1,256,768]{2,1,0:T(8,128)} %param.18) | copy-start | bytes 2359300
  407.5 120.4 %copy-start.1 = (bf16[512,1536]{1,0:T(8,128)(2,1)S(1)}, bf16[512,1536]{1,0:T(8,128)(2,1)}, u32[]{:S(2)}) copy-start(bf16[512,1536]{1,0:T(8,128)(2,1)} %param.16) | copy-start | bytes 4718596
Sparse Core Ops, SparseCore 0:
  9.5 62.7 all-gather.3
  147.4 75.6 reduce-scatter.2
  232.8 16.8 all-gather.5
  251.0 79.9 all-gather.7
  407.6 118.0 reduce-scatter.4
where the time goes:
time: 536 us; the launch traced here: 534 us
  waiting for transfers between devices  385 us (72%)
  local copies, waits for them, and re-layouts  49.6 us (9%)
  matrix products  44.2 us (8%)
  other arithmetic  27.6 us (5%)
  starting transfers between devices  14.6 us (3%)
  between operations  13.4 us (2%)
    reduce_scatter x1, waiting for transfers between devices, per_device(): lax.psum_scatter(rounded.astype(jnp.float32).astype(jnp.bfloat16), 'gy',...  118 us
    reduce_scatter x1, waiting for transfers between devices, per_device(): lax.psum_scatter(jnp.dot(blocks, joined, preferred_element_type=jnp.float...  75.2 us
    all_gather x1, waiting for transfers between devices, per_device(): lax.all_gather(hidden, 'gx', axis=0, tiled=True)  72 us
    all_gather x1, waiting for transfers between devices, per_device(): whole_rows = lax.all_gather(tokens, 'gy', axis=2, tiled=True)  63.7 us
    all_to_all x1, waiting for transfers between devices, per_device(): lax.all_to_all(feedforward_part.astype(jnp.bfloat16), 'gx', split_axis=0,...  24 us
    all_to_all x1, waiting for transfers between devices, per_device(): lax.all_to_all(normed, 'gx', split_axis=1, concat_axis=0, tiled=True)  23.7 us
    dot_general x1, matrix products, per_device(): jnp.dot(blocks, joined, preferred_element_type=jnp.float32)  22.6 us
    dot_general x1, matrix products, per_device(): jnp.dot(lax.all_gather(hidden, 'gx', axis=0, tiled=True), down_weight, pr...  15.6 us
  transfers between devices with their start and end apart: 8, of which 7 were waited for; matrix products, arithmetic and copies ran while one was open for 10% of the time, Pallas kernels for 0%

commit v1 on v0

--- a/solution.py
+++ b/solution.py
@@ -32,7 +32,7 @@
     feedforward_keep,
 ):
     images, seq_len, slice_width = tokens.shape
-    whole_rows = lax.all_gather(tokens, "gy", axis=2, tiled=True)
+    whole_rows = jnp.concatenate(lax.all_gather(tokens, "gy"), axis=2)
     model_width = whole_rows.shape[2]
     own_rows = images * seq_len
     normed = (

time: 536 us -> 541 us (level)
  no operation moved by 1% of the time
where the time goes in v1:
time: 541 us; the launch traced here: 540 us
  waiting for transfers between devices  386 us (71%)
  local copies, waits for them, and re-layouts  53.3 us (10%)
  matrix products  44.2 us (8%)
  other arithmetic  28 us (5%)
  starting transfers between devices  14.6 us (3%)
  between operations  13.4 us (2%)
    reduce_scatter x1, waiting for transfers between devices, per_device(): lax.psum_scatter(rounded.astype(jnp.float32).astype(jnp.bfloat16), 'gy',...  118 us
    reduce_scatter x1, waiting for transfers between devices, per_device(): lax.psum_scatter(jnp.dot(blocks, joined, preferred_element_type=jnp.float...  75.2 us
    all_gather x1, waiting for transfers between devices, per_device(): lax.all_gather(hidden, 'gx', axis=0, tiled=True)  72 us
    all_gather x1, waiting for transfers between devices, per_device(): whole_rows = jnp.concatenate(lax.all_gather(tokens, 'gy'), axis=2)  64.3 us
    all_to_all x1, waiting for transfers between devices, per_device(): lax.all_to_all(feedforward_part.astype(jnp.bfloat16), 'gx', split_axis=0,...  24 us
    all_to_all x1, waiting for transfers between devices, per_device(): lax.all_to_all(normed, 'gx', split_axis=1, concat_axis=0, tiled=True)  23.6 us
    dot_general x1, matrix products, per_device(): jnp.dot(blocks, joined, preferred_element_type=jnp.float32)  22.7 us
    dot_general x1, matrix products, per_device(): jnp.dot(lax.all_gather(hidden, 'gx', axis=0, tiled=True), down_weight, pr...  15.5 us
  transfers between devices with their start and end apart: 8, of which 7 were waited for; matrix products, arithmetic and copies ran while one was open for 10% of the time, Pallas kernels for 0%

profile of v1, /device:TPU:0, one launch (start us, length us, event | category | flops | bytes accessed | tf_op | source)
XLA Modules:
  0.0 539.8 jit_solution(11545328693688601916)
XLA Ops:
  8.0 64.3 %all-gather.9.cloned.1.call-done = bf16[8,256,768]{2,1,0:T(8,128)(2,1)} async-done(((bf16[1,256,768]{2,1,0:T(8,128)(2,1)}), bf16[8,256,768]{2,1,0:T(8,128)(2,1)}) %all-gather.9.cloned.1.call-update) | async-done | bytes 3145744 | tf_op jit(solution)/shard_map/all_gather | solution.py:35
  72.3 4.7 copy.28
  76.9 2.6 convert_element_type.118
  83.6 4.7 all-to-all-start
  88.4 6.7 %copy.30 = bf16[1536,3,512]{0,2,1:T(8,128)(2,1)} copy(bf16[1536,3,512]{2,0,1:T(8,128)(2,1)} %param.12) | data formatting | bytes 9437184 | tf_op args[2]
  95.0 6.6 %copy.31 = bf16[1536,1536]{1,0:T(8,128)(2,1)} copy(bf16[1536,1536]{0,1:T(8,128)(2,1)} %bitcast.81) | data formatting | bytes 9437184 | tf_op jit(solution)/shard_map/reshape | solution.py:47
  101.6 23.6 %all-to-all-done = bf16[256,4,1536]{0,2,1:T(8,128)(2,1)} async-done(((bf16[256,4,1536]{0,2,1:T(8,128)(2,1)}), bf16[256,4,1536]{0,2,1:T(8,128)(2,1)}, u32[]{:S(2)}, u32[]{:S(2)}) %all-to-all-start) | async-done | bytes 3145760 | tf_op jit(solution)/shard_map/all_to_all | solution.py:43
  125.3 4.7 copy.29
  130.0 22.7 %fusion.4 = bf16[1024,4608]{1,0:T(8,128)(2,1)} fusion(bf16[1024,1536]{1,0:T(8,128)(2,1)} %bitcast.84, bf16[1536,3072]{1,0:T(8,128)(2,1)} %param.13, bf16[1536,1536]{1,0:T(8,128)(2,1)} %copy.31), kind=kOutput, calls=%fused_computation.4 | convolution fusion | flops 14528544768 | bytes 26738688 | tf_op jit(solution)/shard_map/dot_general | solution.py:50
  153.3 75.2 %reduce-scatter.3.cloned.1.call-done = bf16[256,4608]{1,0:T(8,128)(2,1)} async-done(((bf16[1024,4608]{1,0:T(8,128)(2,1)}), bf16[256,4608]{1,0:T(8,128)(2,1)}) %reduce-scatter.3.cloned.1.call-update) | async-done | bytes 2359312 | tf_op jit(solution)/shard_map/reduce_scatter | solution.py:49
  238.0 8.6 %fusion.11 = bf16[256,3072]{1,0:T(8,128)(2,1)} fusion(f32[256,4608]{1,0:T(8,128)} %copy-done.3), kind=kLoop, calls=%fused_computation.15 | loop fusion | flops 51118080 | bytes 4718592 | tf_op jit(solution)/shard_map/convert_element_type | solution.py:58
  246.7 8.3 %all-gather.5.cloned.1.call-done = bf16[1024,512]{0,1:T(8,128)(2,1)} async-done(((bf16[256,512]{0,1:T(8,128)(2,1)}), bf16[1024,512]{0,1:T(8,128)(2,1)}) %all-gather.5.cloned.1.call-update) | async-done | bytes 1048592 | tf_op jit(solution)/shard_map/all_gather | solution.py:72
  255.0 4.7 convolution_convert_fusion.1
  259.7 4.7 all-to-all-start.1
  264.4 72.0 %all-gather.7.cloned.1.call-done = bf16[1024,3072]{1,0:T(8,128)(2,1)} async-done(((bf16[256,3072]{1,0:T(8,128)(2,1)}), bf16[1024,3072]{1,0:T(8,128)(2,1)}) %all-gather.7.cloned.1.call-update) | async-done | bytes 6291472 | tf_op jit(solution)/shard_map/all_gather | solution.py:77
  336.4 15.5 %convolution_convert_fusion = bf16[1024,1536]{1,0:T(8,128)(2,1)} fusion(bf16[1024,3072]{1,0:T(8,128)(2,1)} %all-gather.7.cloned.1.call-done, bf16[3072,1536]{1,0:T(8,128)(2,1)} %param.17), kind=kOutput, calls=%fused_computation.11 | convolution fusion | flops 9665249280 | bytes 18874368 | tf_op jit(solution)/shard_map/dot_general | solution.py:76
  352.0 4.9 all-to-all-start.2
  356.9 6.0 %copy.36 = bf16[256,4,1536]{2,1,0:T(4,128)(2,1)} copy(bf16[256,4,1536]{2,0,1:T(8,128)(2,1)} %bitcast.15) | data formatting | bytes 6291456 | tf_op jit(solution)/shard_map/all_to_all | solution.py:82
  362.9 6.9 %stack.9 = bf16[1,256,6144]{2,1,0:T(8,128)(2,1)} reshape(bf16[256,4,1536]{2,1,0:T(4,128)(2,1)} %copy.36) | data formatting | bytes 6291456 | tf_op jit(solution)/shard_map/stack | solution.py:89
  369.8 24.0 %all-to-all-done.2 = bf16[4,256,1536]{2,1,0:T(8,128)(2,1)} async-done(((bf16[4,256,1536]{2,1,0:T(8,128)(2,1)}), bf16[4,256,1536]{2,1,0:T(8,128)(2,1)}, u32[]{:S(2)}, u32[]{:S(2)}) %all-to-all-start.2) | async-done | bytes 3145760 | tf_op jit(solution)/shard_map/all_to_all | solution.py:85
  393.8 6.0 %copy.37 = bf16[256,4,1536]{2,1,0:T(4,128)(2,1)} copy(bf16[256,4,1536]{2,0,1:T(8,128)(2,1)} %bitcast.17) | data formatting | bytes 6291456 | tf_op jit(solution)/shard_map/all_to_all | solution.py:85
  399.8 6.9 %stack.10 = bf16[1,256,6144]{2,1,0:T(8,128)(2,1)} reshape(bf16[256,4,1536]{2,1,0:T(4,128)(2,1)} %copy.37) | data formatting | bytes 6291456 | tf_op jit(solution)/shard_map/stack | solution.py:89
  406.7 6.1 %pad_maximum_fusion = bf16[2,256,6144]{2,1,0:T(8,128)(2,1)} fusion(bf16[1,256,6144]{2,1,0:T(8,128)(2,1)} %stack.10, bf16[1,256,6144]{2,1,0:T(8,128)(2,1)} %stack.9), kind=kLoop, calls=%fused_computation.5 | loop fusion | flops 3145728 | bytes 12582912 | tf_op jit(solution)/shard_map/stack | solution.py:89
  412.9 118.2 %reduce-scatter.5.cloned.1.call-done = bf16[2,256,768]{2,1,0:T(8,128)(2,1)} async-done(((bf16[2,256,6144]{2,1,0:T(8,128)(2,1)}), bf16[2,256,768]{2,1,0:T(8,128)(2,1)}) %reduce-scatter.5.cloned.1.call-update) | async-done | bytes 786448 | tf_op jit(solution)/shard_map/reduce_scatter | solution.py:91
  (60 shorter events, 18.0 us)
Async XLA Ops:
  6.5 248.4 %copy-start = (bf16[512,1536]{1,0:T(8,128)(2,1)S(1)}, bf16[512,1536]{1,0:T(8,128)(2,1)}, u32[]{:S(2)}) copy-start(bf16[512,1536]{1,0:T(8,128)(2,1)} %param.16) | copy-start | bytes 4718596
  6.5 65.7 %all-gather.9.cloned.1.call-start = ((), (), s32[]{:S(2)}) async-start(), calls=%async_computation.9 | async-start | bytes 3538944 | tf_op jit(solution)/shard_map/all_gather | solution.py:35
  76.9 2.8 copy-start.2
  83.6 41.7 %all-to-all-start = ((bf16[256,4,1536]{0,2,1:T(8,128)(2,1)}), bf16[256,4,1536]{0,2,1:T(8,128)(2,1)}, u32[]{:S(2)}, u32[]{:S(2)}) async-start(bf16[256,4,1536]{0,2,1:T(8,128)(2,1)} %multiply_convert_fusion), calls=%async_computation | async-start | bytes 6291456 | tf_op jit(solution)/shard_map/all_to_all | solution.py:43
  88.3 140.2 %reduce-scatter.3.cloned.1.call-start = ((), (), s32[]{:S(2)}) async-start(), calls=%async_computation.5 | async-start | bytes 11796480 | tf_op jit(solution)/shard_map/reduce_scatter | solution.py:49
  152.6 0.7 copy-start.7
  152.6 0.7 copy-start.8
  152.6 102.3 %all-gather.5.cloned.1.call-start = ((), (), s32[]{:S(2)}) async-start(), calls=%async_computation.6 | async-start | bytes 1310720 | tf_op jit(solution)/shard_map/all_gather | solution.py:72
  229.6 2.5 slice-start
  234.5 2.1 copy-start.3
  238.0 98.4 %all-gather.7.cloned.1.call-start = ((), (), s32[]{:S(2)}) async-start(), calls=%async_computation.7 | async-start | bytes 7864320 | tf_op jit(solution)/shard_map/all_gather | solution.py:77
  259.7 92.3 %all-to-all-start.1 = ((bf16[4,256,1536]{2,1,0:T(8,128)(2,1)}), bf16[4,256,1536]{2,1,0:T(8,128)(2,1)}, u32[]{:S(2)}, u32[]{:S(2)}) async-start(bf16[4,256,1536]{2,1,0:T(8,128)(2,1)} %bitcast.83), calls=%async_computation.2 | async-start | bytes 6291456 | tf_op jit(solution)/shard_map/all_to_all | solution.py:82
  352.0 41.8 %all-to-all-start.2 = ((bf16[4,256,1536]{2,1,0:T(8,128)(2,1)}), bf16[4,256,1536]{2,1,0:T(8,128)(2,1)}, u32[]{:S(2)}, u32[]{:S(2)}) async-start(bf16[4,256,1536]{2,1,0:T(8,128)(2,1)} %bitcast.82), calls=%async_computation.3 | async-start | bytes 6291456 | tf_op jit(solution)/shard_map/all_to_all | solution.py:85
  356.8 174.2 %reduce-scatter.5.cloned.1.call-start = ((), (), s32[]{:S(2)}) async-start(), calls=%async_computation.8 | async-start | bytes 7077888 | tf_op jit(solution)/shard_map/reduce_scatter | solution.py:91
  412.8 119.4 %copy-start.4 = (bf16[1,256,768]{2,1,0:T(8,128)(2,1)S(1)}, bf16[1,256,768]{2,1,0:T(8,128)(2,1)}, u32[]{:S(2)}) copy-start(bf16[1,256,768]{2,1,0:T(8,128)(2,1)} %param.10) | copy-start | bytes 1179652
  412.8 119.5 %copy-start.5 = (s32[1,256,768]{2,1,0:T(8,128)S(1)}, s32[1,256,768]{2,1,0:T(8,128)}, u32[]{:S(2)}) copy-start(s32[1,256,768]{2,1,0:T(8,128)} %param.19) | copy-start | bytes 2359300
  412.8 119.5 %copy-start.6 = (s32[1,256,768]{2,1,0:T(8,128)S(1)}, s32[1,256,768]{2,1,0:T(8,128)}, u32[]{:S(2)}) copy-start(s32[1,256,768]{2,1,0:T(8,128)} %param.18) | copy-start | bytes 2359300
  412.9 120.4 %copy-start.1 = (bf16[512,1536]{1,0:T(8,128)(2,1)S(1)}, bf16[512,1536]{1,0:T(8,128)(2,1)}, u32[]{:S(2)}) copy-start(bf16[512,1536]{1,0:T(8,128)(2,1)} %param.16) | copy-start | bytes 4718596
Sparse Core Ops, SparseCore 0:
  9.5 62.7 all-gather.8
  152.8 75.6 reduce-scatter.2
  238.1 16.8 all-gather.4
  256.4 79.9 all-gather.6
  413.0 117.9 reduce-scatter.4
